TPU v7x, 512 devices: a whole 4x8x8 slice. The times are simulated.
512 devices in a mesh: dp: 32 (over x, y_hi, core), fsdp: 16 (over y_lo, z).
Axes of the slice: x: 4, y: 8 (y_hi: 4, y_lo: 2; y = y_hi * 2 + y_lo), z: 8, core: 2. Of those that a mesh axis runs over, the one named last changes fastest.
Arguments:
- hidden: bfloat16 [4, 2048, 16, 4096], P(None, 'dp', 'fsdp'), may hold values from -6 to 6
- frozen_query_rows: bfloat16 [4, 2048, 16, 2048], P(None, 'dp', 'fsdp'), may hold values from -10 to 10
- output_gradient: bfloat16 [4, 2048, 16, 2048], P(None, 'dp', 'fsdp'), may hold values from -6 to 6
- token_log_ratio: float32 [4, 2048, 16], P(None, 'dp', 'fsdp'), may hold values from -0.15625 to 0.15625
- lengths: int32 [4], replicated, may hold values from 1 to 32768, as said below
- response_win_probability: float32 [4], replicated, may hold values from 0.05 to 0.95
- cached_prompt_keys: bfloat16 [1024, 512], P('fsdp'), may hold values from -7.5 to 7.5
- cached_prompt_values: bfloat16 [1024, 512], P('fsdp'), may hold values from -6 to 6
- adapter_down_factor: bfloat16 [4096, 64], P('fsdp'), may hold values from -0.09375 to 0.09375
- adapter_up_factor: bfloat16 [64, 2048], P(None, 'fsdp'), may hold values from -0.125 to 0.125
- attention_norm_gain: bfloat16 [4096], P('fsdp'), may hold values from 0.5 to 1.5
Outputs:
- grad_down: float32 [4096, 64], P('fsdp')
- grad_up: float32 [64, 2048], P(None, 'fsdp')
- seq_ratio: float32 [4], replicated
Inputs may be any that keep to these rules, and one draw needn't show every extreme that they name: The lengths sum to 65472 and the longest is exactly 32768.
All inputs are finite; a program needn't handle non-finite values.
Results may differ from a plain program's by a relative error of at most 0.012.
Values may be sent and summed in bfloat16 or wider, within the bound.
A program may use at most 128 MiB of HBM per device.

v0:
```python
import math

import jax
import jax.numpy as jnp
from jax import lax
from jax.sharding import PartitionSpec as P

HEAD_SIZE = 128
QUERY_HEADS = 16
KEY_VALUE_HEADS = 4


target_scale = 1.0
norm_epsilon = 1e-05


def attend(query_vectors, cotangent, key_rows, value_rows):
    row_count = query_vectors.shape[0]
    queries_per_group = QUERY_HEADS // KEY_VALUE_HEADS
    score_scale = 1.0 / math.sqrt(HEAD_SIZE)
    pieces = []
    for shared_key_head in range(KEY_VALUE_HEADS):
        head_start = shared_key_head * queries_per_group * HEAD_SIZE
        head_stop = head_start + queries_per_group * HEAD_SIZE
        head_query = query_vectors[:, head_start:head_stop].reshape(
            row_count, queries_per_group, HEAD_SIZE
        )
        head_grad = cotangent[:, head_start:head_stop].reshape(
            row_count, queries_per_group, HEAD_SIZE
        )
        head_key = key_rows[:, shared_key_head * HEAD_SIZE : (shared_key_head + 1) * HEAD_SIZE]
        head_value = value_rows[:, shared_key_head * HEAD_SIZE : (shared_key_head + 1) * HEAD_SIZE]
        scores = (
            jnp.einsum("nhd,jd->nhj", head_query, head_key, preferred_element_type=jnp.float32)
            * score_scale
        )
        row_top = jnp.max(scores, axis=2, keepdims=True)
        exponent = jnp.exp(scores - row_top)
        row_total = jnp.sum(exponent, axis=2, keepdims=True)
        weights = exponent.astype(jnp.bfloat16)
        mixed_out = (
            jnp.einsum("nhj,jd->nhd", weights, head_value, preferred_element_type=jnp.float32)
            / row_total
        )
        inner_prod = jnp.sum(head_grad.astype(jnp.float32) * mixed_out, axis=2, keepdims=True)
        grad_prob = jnp.einsum(
            "nhd,jd->nhj", head_grad, head_value, preferred_element_type=jnp.float32
        )
        grad_score = (weights.astype(jnp.float32) / row_total * (grad_prob - inner_prod)).astype(
            jnp.bfloat16
        )
        query_gradient = (
            jnp.einsum("nhj,jd->nhd", grad_score, head_key, preferred_element_type=jnp.float32)
            * score_scale
        )
        pieces.append(query_gradient.reshape(row_count, queries_per_group * HEAD_SIZE))
    return jnp.concatenate(pieces, axis=1).astype(jnp.bfloat16)


def body(
    hidden,
    frozen_query_rows,
    output_gradient,
    token_log_ratio,
    lengths,
    response_win_probability,
    cached_prompt_keys,
    cached_prompt_values,
    adapter_down_factor,
    adapter_up_factor,
    attention_norm_gain,
):
    fsdp_count = lax.axis_size("fsdp")
    dp_index = lax.axis_index("dp")
    fsdp_index = lax.axis_index("fsdp")
    responses, per_device, single, feature_count = hidden.shape
    home_rows = responses * per_device
    local_rows = jnp.arange(per_device, dtype=jnp.int32)
    position = (dp_index * per_device + local_rows) * fsdp_count + fsdp_index
    is_valid = position[None, :] < lengths[:, None]
    partial_value = jnp.sum(jnp.where(is_valid, token_log_ratio[:, :, 0], 0.0), axis=1)
    seq_ratio = lax.psum(partial_value, ("dp", "fsdp"))
    weighting = 2.0 * (seq_ratio - target_scale * (response_win_probability - 0.5)) / responses
    down_full, up_full, gain_full = (
        lax.all_gather(adapter_down_factor, "fsdp", axis=0, tiled=True),
        lax.all_gather(adapter_up_factor, "fsdp", axis=1, tiled=True),
        lax.all_gather(attention_norm_gain, "fsdp", axis=0, tiled=True),
    )
    key_rows, value_rows = (
        lax.all_gather(cached_prompt_keys, "fsdp", axis=0, tiled=True),
        lax.all_gather(cached_prompt_values, "fsdp", axis=0, tiled=True),
    )
    widened = hidden.reshape(home_rows, feature_count).astype(jnp.float32)
    inverse = lax.rsqrt(jnp.mean(widened * widened, axis=1, keepdims=True) + norm_epsilon)
    normed_input = (widened * inverse * gain_full.astype(jnp.float32)).astype(jnp.bfloat16)
    lowrank_hidden = jnp.dot(normed_input, down_full, preferred_element_type=jnp.float32).astype(
        jnp.bfloat16
    )
    row_mask = is_valid.reshape(home_rows)
    row_coef = jnp.repeat(weighting, per_device)
    base_rows = frozen_query_rows.reshape(home_rows, -1)
    cotangent = jnp.where(
        row_mask[:, None],
        row_coef[:, None] * output_gradient.reshape(home_rows, -1).astype(jnp.float32),
        0.0,
    ).astype(jnp.bfloat16)
    query_vectors = (
        base_rows.astype(jnp.float32)
        + jnp.dot(lowrank_hidden, up_full, preferred_element_type=jnp.float32)
    ).astype(jnp.bfloat16)
    query_gradient = attend(query_vectors, cotangent, key_rows, value_rows)
    up_term = jnp.dot(lowrank_hidden.T, query_gradient, preferred_element_type=jnp.float32)
    gradient_lowrank = jnp.dot(
        query_gradient, up_full.T, preferred_element_type=jnp.float32
    ).astype(jnp.bfloat16)
    down_term = jnp.dot(normed_input.T, gradient_lowrank, preferred_element_type=jnp.float32)
    down_sum, up_sum = lax.psum((down_term, up_term), ("dp", "fsdp"))
    down_factor_part = adapter_down_factor.shape[0]
    up_factor_part = adapter_up_factor.shape[1]
    grad_down = lax.dynamic_slice_in_dim(
        down_sum, fsdp_index * down_factor_part, down_factor_part, 0
    )
    grad_up = lax.dynamic_slice_in_dim(up_sum, fsdp_index * up_factor_part, up_factor_part, 1)
    return (grad_down, grad_up, seq_ratio)


def solution(mesh):
    in_specs = (
        P(None, "dp", "fsdp", None),
        P(None, "dp", "fsdp", None),
        P(None, "dp", "fsdp", None),
        P(None, "dp", "fsdp"),
        P(),
        P(),
        P("fsdp", None),
        P("fsdp", None),
        P("fsdp", None),
        P(None, "fsdp"),
        P("fsdp"),
    )
    out_specs = (P("fsdp", None), P(None, "fsdp"), P())
    return jax.shard_map(body, mesh=mesh, in_specs=in_specs, out_specs=out_specs, check_vma=False)
```

profile of v0, /device:TPU:1, one launch (start us, length us, event | category | flops | bytes accessed | tf_op | source)
XLA Modules:
  0.0 573.5 jit_solution(2248930495816452318)
XLA Ops:
  9.6 107.1 %psum.21 = f32[4]{0:T(128)S(1)} all-reduce(f32[4]{0:T(128)S(1)} %get-tuple-element.5), channel_id=1, replica_groups=mesh['dp'=32,'fsdp'=16] {'dp','fsdp'}, use_global_device_ids=true, to_apply=%region_4.5 | all-reduce | flops 4 | bytes 32 | tf_op jit(solution)/shard_map/psum | solution.py:82
  118.3 2.1 multiply_reduce_fusion
  120.5 24.9 %all-gather = bf16[16,1,256]{2,1,0:T(2,128)(2,1)S(1)} all-gather(bf16[1,1,256]{2,1,0:T(2,128)(2,1)S(1)} %reshape.122), channel_id=1, replica_groups=mesh['dp'=32,'fsdp'=16] {'fsdp'}, dimensions={0}, use_global_device_ids=true | all-gather | bytes 8704 | tf_op jit(solution)/shard_map/all_gather | solution.py:87
  145.4 2.2 fusion.1
  148.0 1.3 slice_bitcast_fusion.35
  149.3 1.7 reshape.117
  151.0 1.7 reshape.114
  152.7 1.7 reshape.111
  155.2 24.0 %all_gather.17 = bf16[64,2048]{1,0:T(8,128)(2,1)S(1)} all-gather(bf16[64,128]{1,0:T(8,128)(2,1)S(1)} %copy-done.17), channel_id=1, replica_groups=mesh['dp'=32,'fsdp'=16] {'fsdp'}, dimensions={1}, use_global_device_ids=true | all-gather | bytes 278528 | tf_op jit(solution)/shard_map/all_gather | solution.py:86
  179.2 27.2 %all_gather.16 = bf16[4096,64]{0,1:T(8,128)(2,1)S(1)} all-gather(bf16[256,64]{0,1:T(8,128)(2,1)S(1)} %copy-done.16), channel_id=1, replica_groups=mesh['dp'=32,'fsdp'=16] {'fsdp'}, dimensions={0}, use_global_device_ids=true | all-gather | bytes 557056 | tf_op jit(solution)/shard_map/all_gather | solution.py:85
  208.7 1.7 multiply_reduce_fusion.4
  210.5 2.0 copy-done
  213.6 3.0 fusion.39
  218.1 1.9 multiply_reduce_fusion.1
  220.0 1.9 copy-done.1
  223.7 3.1 fusion.30
  228.2 1.8 multiply_reduce_fusion.2
  230.0 2.0 copy-done.2
  233.7 3.1 fusion.33
  238.3 1.8 multiply_reduce_fusion.3
  240.1 1.9 copy-done.3
  242.0 1.1 fusion.4
  244.0 3.1 fusion.36
  248.5 4.8 fusion.21
  253.4 4.8 fusion.24
  258.2 4.8 fusion.23
  263.0 4.8 fusion.22
  267.8 3.6 fusion.25
  271.5 2.2 fusion.70
  273.7 290.4 %all-reduce.3.cloned.1.call-done = (f32[4096,64]{0,1:T(8,128)}, f32[64,2048]{1,0:T(8,128)}) async-done(((f32[4096,64]{0,1:T(8,128)}, f32[64,2048]{1,0:T(8,128)}), (f32[4096,64]{0,1:T(8,128)}, f32[64,2048]{1,0:T(8,128)})) %all-reduce.3.cloned.1.call-update) | async-done | bytes 1572880 | tf_op jit(solution)/shard_map/psum | solution.py:117
  564.1 1.5 constant_dynamic-slice_fusion.1
  565.6 1.4 constant_dynamic-slice_fusion
  (98 shorter events, 18.6 us)
Async XLA Ops:
  7.2 140.4 %copy-start.6 = (bf16[4,64,1,2048]{3,1,2,0:T(8,128)(2,1)S(1)}, bf16[4,64,1,2048]{3,1,2,0:T(8,128)(2,1)}, u32[]{:S(2)}) copy-start(bf16[4,64,1,2048]{3,1,2,0:T(8,128)(2,1)} %param.13) | copy-start | bytes 3145732
  7.2 201.6 %all-gather.4.cloned.1.call-start = ((), (), s32[]{:S(2)}) async-start(), calls=%async_computation | async-start | bytes 1114112 | tf_op jit(solution)/shard_map/all_gather | solution.py:90
  7.9 205.7 %all-gather.6.cloned.1.call-start = ((), (), s32[]{:S(2)}) async-start(), calls=%async_computation.1 | async-start | bytes 1114112 | tf_op jit(solution)/shard_map/all_gather | solution.py:91
  8.7 555.5 %all-reduce.3.cloned.1.call-start = ((), (), s32[]{:S(2)}) async-start(), calls=%async_computation.2 | async-start | bytes 3145728 | tf_op jit(solution)/shard_map/psum | solution.py:117
  116.7 3.7 copy-start.31
  147.6 7.6 %copy-start.17 = (bf16[64,128]{1,0:T(8,128)(2,1)S(1)}, bf16[64,128]{1,0:T(8,128)(2,1)}, u32[]{:S(2)}) copy-start(bf16[64,128]{1,0:T(8,128)(2,1)} %param.20) | copy-start | bytes 49156
  147.6 31.6 %copy-start.16 = (bf16[256,64]{0,1:T(8,128)(2,1)S(1)}, bf16[256,64]{0,1:T(8,128)(2,1)}, u32[]{:S(2)}) copy-start(bf16[256,64]{0,1:T(8,128)(2,1)} %param.19) | copy-start | bytes 98308
  148.0 59.3 %copy-start.5 = (bf16[4,64,1,2048]{3,1,2,0:T(8,128)(2,1)S(1)}, bf16[4,64,1,2048]{3,1,2,0:T(8,128)(2,1)}, u32[]{:S(2)}) copy-start(bf16[4,64,1,2048]{3,1,2,0:T(8,128)(2,1)} %param.12) | copy-start | bytes 3145732
  210.5 2.0 copy-start
  212.5 4.2 copy-start.10
  213.4 6.6 %copy-start.18 = (f32[256,4]{0,1:T(4,128)}, f32[256,4]{0,1:T(4,128)S(1)}, u32[]{:S(2)}) copy-start(f32[256,4]{0,1:T(4,128)S(1)} %fusion.2) | copy-start | bytes 12292
  218.1 5.6 copy-start.4
  220.0 1.9 copy-start.1
  222.8 0.8 copy-start.19
  223.7 3.1 copy-start.9
  223.7 3.1 copy-start.11
  230.0 2.0 copy-start.2
  233.7 3.1 copy-start.8
  233.7 3.1 copy-start.12
  240.1 1.9 copy-start.3
  244.0 3.1 copy-start.7
  244.0 3.1 copy-start.13
  248.5 4.8 copy-start.20
  248.5 4.8 copy-start.25
  253.4 4.8 copy-start.22
  253.4 4.8 copy-start.26
  258.2 4.8 copy-start.24
  258.2 4.8 copy-start.27
  267.8 3.7 copy-start.15
  267.8 3.7 copy-start.28
  267.8 3.7 copy-start.29
  267.8 3.7 copy-start.30
  (3 other events, 2.2 us)
Sparse Core Ops, SparseCore 0:
  10.1 67.9 all-gather.3
  80.1 70.1 all-gather.5
  273.8 290.2 all-reduce.2
where the time goes:
time: 575 us; the launch traced here: 573 us
  waiting for transfers between devices  292 us (51%)
  blocking collectives  183 us (32%)
  matrix products  45.8 us (8%)
  local copies, waits for them, and re-layouts  25.3 us (4%)
  between operations  14.1 us (2%)
  other arithmetic  13.1 us (2%)
    psum x1, waiting for transfers between devices, body(): down_sum, up_sum = lax.psum((down_term, up_term), ('dp', 'fsdp'))  290 us
    psum x1, blocking collectives, body(): seq_ratio = lax.psum(partial_value, ('dp', 'fsdp'))  107 us
    all_gather x1, blocking collectives, body(): lax.all_gather(adapter_down_factor, 'fsdp', axis=0, tiled=True)  27.2 us
    all_gather x1, blocking collectives, body(): lax.all_gather(attention_norm_gain, 'fsdp', axis=0, tiled=True)  24.9 us
    all_gather x1, blocking collectives, body(): lax.all_gather(adapter_up_factor, 'fsdp', axis=1, tiled=True)  24 us
    dot_general x4, matrix products, attend(): jnp.einsum('nhj,jd->nhd', grad_score, head_key, preferred_element_type=jn...  19.2 us
    dot_general x4, matrix products, attend(): jnp.einsum('nhj,jd->nhd', weights, head_value, preferred_element_type=jnp...  12.3 us
  transfers between devices with their start and end apart: 3, of which 1 were waited for; matrix products, arithmetic and copies ran while one was open for 3% of the time, Pallas kernels for 0%

commit v1 on v0

v1 whole, which is shorter than its diff:
```python
import math

import jax
import jax.numpy as jnp
from jax import lax
from jax.experimental import pallas as pl
from jax.experimental.pallas import tpu as pltpu
from jax.sharding import PartitionSpec as P

MESH = pl.DeviceIdType.MESH
HEAD = 128
HEADS = 16
GROUPS = 4
RANK = 64
WIDTH = 4096
PROMPT = 1024
RESP = 4
ROWS = 256
FS = 16
NZ, NX, NYH = 8, 4, 4
PROWS, PCOLS = 40, 384
EPS = 1e-05
BF, F32 = jnp.bfloat16, jnp.float32


def place():
    dp = lax.axis_index("dp")
    fs = lax.axis_index("fsdp")
    core = lax.rem(dp, 2)
    yh = lax.rem(dp // 2, NYH)
    x = dp // (2 * NYH)
    z = lax.rem(fs, NZ)
    yl = fs // NZ
    return x, yh, core, yl, z


def dev(x, yh, core, yl, z):
    return ((x * NYH + yh) * 2 + core, yl * NZ + z)


def send(src, dst, ssem, rsem, where):
    copy = pltpu.make_async_remote_copy(
        src_ref=src, dst_ref=dst, send_sem=ssem, recv_sem=rsem, device_id=where, device_id_type=MESH
    )
    copy.start()
    return copy


def greet(peers):
    barrier = pltpu.get_barrier_semaphore()
    for where in peers:
        pl.semaphore_signal(barrier, inc=1, device_id=where, device_id_type=MESH)
    pl.semaphore_wait(barrier, len(peers))


CHUNKS = 5


def gather_kernel(
    lengths_ref, tlr_ref, k_ref, v_ref, down_ref, up_ref, gain_ref,
    seq_ref, kv_ref, par_ref,
    kv, par, tot0, tot1, tot2, tot3,
    load_sem, zs_sem, zr_sem, ys_sem, yr_sem, cs_sem, cr_sem, ts_sem, tr_sem, out_sem,
):
    x, yh, core, yl, z = place()
    me = yl * NZ + z
    y = yh * 2 + yl
    other = 1 - core
    loads = []
    for g in range(GROUPS):
        cols = pl.ds(g * HEAD, HEAD)
        for kind, src in ((0, k_ref), (1, v_ref)):
            loads.append(pltpu.make_async_copy(src.at[:, cols], kv.at[kind, g, me], load_sem.at[kind * GROUPS + g]))
    for half in range(2):
        rows = pl.ds(half * 32, 32)
        loads.append(pltpu.make_async_copy(down_ref.at[rows, :], par.at[half, me, pl.ds(0, 32), pl.ds(0, 256)], load_sem.at[8 + 3 * half]))
        loads.append(pltpu.make_async_copy(up_ref.at[rows, :], par.at[half, me, pl.ds(0, 32), pl.ds(256, 128)], load_sem.at[9 + 3 * half]))
        loads.append(pltpu.make_async_copy(gain_ref, par.at[half, me, pl.ds(32, 8), :], load_sem.at[10 + 3 * half]))
    for copy in loads:
        copy.start()

    place_row = lax.broadcasted_iota(jnp.int32, (RESP, 64), 1)
    resp = lax.broadcasted_iota(jnp.int32, (RESP, 64), 0)
    position = (((x * NYH + yh) * 2 + core) * 64 + place_row) * FS + me
    limit = jnp.full((RESP, 64), lengths_ref[0], jnp.int32)
    for r in range(1, RESP):
        limit = jnp.where(resp == r, lengths_ref[r], limit)
    mine = jnp.sum(jnp.where(position < limit, tlr_ref[...], 0.0), axis=1, keepdims=True)
    tot0[core] = jnp.zeros((8, 128), F32)
    tot0[core, pl.ds(0, RESP), :] = jnp.broadcast_to(mine, (RESP, 128))

    peers = [dev(x, yh, other, yl, z)]
    peers += [dev(lax.rem(x + d, NX), yh, core, yl, z) for d in range(1, NX)]
    peers += [dev(x, lax.rem(y + d, 8) // 2, core, lax.rem(lax.rem(y + d, 8), 2), z) for d in range(1, 8)]
    peers += [dev(x, yh, core, yl, lax.rem(z + d, NZ)) for d in range(1, NZ)]
    greet(peers)
    for copy in loads:
        copy.wait()

    right = dev(x, yh, core, yl, lax.rem(z + 1, NZ))
    left = dev(x, yh, core, yl, lax.rem(z + NZ - 1, NZ))
    flip = dev(x, yh, core, 1 - yl, z)
    twin = dev(x, yh, other, yl, z)
    waits = []

    def piece(kind, f, chunk):
        return par.at[kind, f] if chunk == 0 else kv.at[kind, chunk - 1, f]

    def go(where, kind, f, chunk, ssem, rsem):
        ref = piece(kind, f, chunk)
        waits.append(send(ref, ref, ssem, rsem, where))

    def arrive(kind, f, chunk, rsem):
        ref = piece(kind, f, chunk)
        pltpu.make_async_remote_copy(
            src_ref=ref, dst_ref=ref, send_sem=rsem, recv_sem=rsem, device_id=twin, device_id_type=MESH
        ).wait_recv()

    def twin_send(b, zo, chunk, slot):
        go(twin, core, b * NZ + zo, chunk, cs_sem.at[slot, chunk], cr_sem.at[slot, chunk])

    sums = [
        (tot0, 2, core, lambda d: twin, 0),
        (tot1, NX, x, lambda d: dev(lax.rem(x + d, NX), yh, core, yl, z), 1),
        (tot2, 8, y, lambda d: dev(x, lax.rem(y + d, 8) // 2, core, lax.rem(lax.rem(y + d, 8), 2), z), 4),
        (tot3, NZ, z, lambda d: dev(x, yh, core, yl, lax.rem(z + d, NZ)), 11),
    ]

    def sum_start(i):
        buf, n, at, who, base = sums[i]
        return [send(buf.at[at], buf.at[at], ts_sem.at[base + d - 1], tr_sem.at[base + d - 1], who(d)) for d in range(1, n)]

    def sum_end(i, copies):
        buf, n, at, who, base = sums[i]
        for copy in copies:
            copy.wait()
        total = buf[0]
        for j in range(1, n):
            total = total + buf[j]
        return total

    sum_copies = sum_start(0)
    for t in range(CHUNKS + 4):
        for chunk in range(CHUNKS):
            step = t - chunk
            if step == 0:
                go(flip, core, me, chunk, ys_sem.at[chunk], yr_sem.at[chunk])
                for b, side in ((0, right), (1, left)):
                    go(side, core, me, chunk, zs_sem.at[b, 0, 0, chunk], zr_sem.at[b, 0, 0, chunk])
                arrive(core, (1 - yl) * NZ + z, chunk, yr_sem.at[chunk])
                for b, side in ((0, right), (1, left)):
                    go(side, core, (1 - yl) * NZ + z, chunk, zs_sem.at[b, 0, 1, chunk], zr_sem.at[b, 0, 1, chunk])
                twin_send(1 - yl, z, chunk, 1)
            elif 1 <= step <= 4:
                for lane in range(2):
                    b = yl if lane == 0 else 1 - yl
                    for way, side in ((0, right), (1, left)):
                        if step == 4 and (lane != way):
                            continue
                        zo = lax.rem(z + NZ - step, NZ) if way == 0 else lax.rem(z + step, NZ)
                        f = b * NZ + zo
                        arrive(core, f, chunk, zr_sem.at[way, step - 1, lane, chunk])
                        if step < 3 or (step == 3 and lane == way):
                            go(side, core, f, chunk, zs_sem.at[way, step, lane, chunk], zr_sem.at[way, step, lane, chunk])
                        twin_send(b, zo, chunk, 2 + ((step - 1) * 2 + lane) * 2 + way if step < 4 else 14 + lane)
        if t == 1:
            tot1[x] = sum_end(0, sum_copies)
            sum_copies = sum_start(1)
        if t == 3:
            tot2[y] = sum_end(1, sum_copies)
            sum_copies = sum_start(2)
        if t == 5:
            tot3[z] = sum_end(2, sum_copies)
            sum_copies = sum_start(3)
    seq_ref[...] = sum_end(3, sum_copies)
    for copy in waits:
        copy.wait_send()
    for chunk in range(CHUNKS):
        arrive(other, (1 - yl) * NZ + z, chunk, cr_sem.at[1, chunk])
        for step in range(1, 5):
            for lane in range(2):
                b = yl if lane == 0 else 1 - yl
                for way in range(2):
                    if step == 4 and (lane != way):
                        continue
                    zo = lax.rem(z + NZ - step, NZ) if way == 0 else lax.rem(z + step, NZ)
                    slot = 2 + ((step - 1) * 2 + lane) * 2 + way if step < 4 else 14 + lane
                    arrive(other, b * NZ + zo, chunk, cr_sem.at[slot, chunk])
    outs = [pltpu.make_async_copy(kv, kv_ref, out_sem.at[0]), pltpu.make_async_copy(par, par_ref, out_sem.at[1])]
    for copy in outs:
        copy.start()
    for copy in outs:
        copy.wait()


def gather(lengths, tlr, k, v, down_t, up, gain8):
    any_ = pl.BlockSpec(memory_space=pl.ANY)
    vmem = pl.BlockSpec(memory_space=pltpu.VMEM)
    dma = pltpu.SemaphoreType.DMA
    return pl.pallas_call(
        gather_kernel,
        out_shape=(
            jax.ShapeDtypeStruct((8, 128), F32),
            jax.ShapeDtypeStruct((2, GROUPS, FS, 64, HEAD), BF),
            jax.ShapeDtypeStruct((2, FS, PROWS, PCOLS), BF),
        ),
        in_specs=[pl.BlockSpec(memory_space=pltpu.SMEM), vmem, any_, any_, any_, any_, any_],
        out_specs=(vmem, any_, any_),
        scratch_shapes=[
            pltpu.VMEM((2, GROUPS, FS, 64, HEAD), BF),
            pltpu.VMEM((2, FS, PROWS, PCOLS), BF),
            pltpu.VMEM((2, 8, 128), F32),
            pltpu.VMEM((NX, 8, 128), F32),
            pltpu.VMEM((8, 8, 128), F32),
            pltpu.VMEM((NZ, 8, 128), F32),
            dma((14,)),
            dma((2, 4, 2, CHUNKS)),
            dma((2, 4, 2, CHUNKS)),
            dma((CHUNKS,)),
            dma((CHUNKS,)),
            dma((16, CHUNKS)),
            dma((16, CHUNKS)),
            dma((18,)),
            dma((18,)),
            dma((2,)),
        ],
        compiler_params=pltpu.CompilerParams(collective_id=0, has_side_effects=True),
        name="gather",
    )(lengths, tlr, k, v, down_t, up, gain8)


NT = (((1,), (1,)), ((), ()))
TN = (((0,), (0,)), ((), ()))


def mm(a, b, dims=(((1,), (0,)), ((), ()))):
    return lax.dot_general(a, b, dims, preferred_element_type=F32)


def math_kernel(
    lengths_ref, win_ref, dp_ref, seq_ref, hidden_ref, frozen_ref, grad_ref, kv_ref, par_ref,
    out_ref,
    normed, low_ref, low32, inv_ref, coef_ref, glow_ref,
):
    dp, fs = dp_ref[0], dp_ref[1]
    scale = 1.0 / math.sqrt(HEAD)
    place_row = lax.broadcasted_iota(jnp.int32, (64, 1), 0)
    position = (dp * 64 + place_row) * FS + fs
    for r in range(RESP):
        seq = seq_ref[pl.ds(r, 1), pl.ds(0, 1)]
        weight = 2.0 * (seq - (win_ref[r] - 0.5)) / RESP
        coef_ref[pl.ds(r * 64, 64), :] = jnp.where(position < lengths_ref[r], jnp.broadcast_to(weight, (64, 1)), 0.0) * scale

    square = jnp.zeros((ROWS, 256), F32)
    for f in range(FS):
        part = hidden_ref[:, pl.ds(f * 256, 256)].astype(F32)
        square = square + part * part
    inv_ref[...] = lax.rsqrt(jnp.sum(square, axis=1, keepdims=True) * (1.0 / WIDTH) + EPS)
    low32[...] = jnp.zeros_like(low32)

    def norm_step(f, carry):
        cols = pl.ds(pl.multiple_of(f * 256, 256), 256)
        part = hidden_ref[:, cols].astype(F32)
        gain = par_ref[0, f, pl.ds(32, 8), pl.ds(0, 256)].astype(F32)[0:1]
        value = (part * inv_ref[...] * gain).astype(BF)
        normed[:, cols] = value
        down = par_ref[:, f, pl.ds(0, 32), pl.ds(0, 256)].reshape(RANK, 256)
        low32[...] += mm(value, down, NT)
        return carry

    lax.fori_loop(0, FS, norm_step, 0)
    low_ref[...] = low32[...].astype(BF)
    glow_ref[...] = jnp.zeros_like(glow_ref)

    def head_step(h, carry):
        g = h // (HEADS // GROUPS)
        cols = pl.ds(pl.multiple_of(h * HEAD, HEAD), HEAD)
        up = par_ref[:, h, pl.ds(0, 32), pl.ds(256, HEAD)].reshape(RANK, HEAD)
        query = (frozen_ref[:, cols].astype(F32) + mm(low_ref[...], up)).astype(BF)
        keys = kv_ref[0, g].reshape(PROMPT, HEAD)
        values = kv_ref[1, g].reshape(PROMPT, HEAD)
        scores = mm(query, keys, NT)
        top = jnp.max(scores, axis=1, keepdims=True)
        c = scale * math.log2(math.e)
        expo = jnp.exp2((scores - top) * c)
        total = jnp.sum(expo, axis=1, keepdims=True)
        weights = expo.astype(BF)
        grad_prob = mm(grad_ref[:, cols], values, NT)
        wide = weights.astype(F32)
        inner = jnp.sum(wide * grad_prob, axis=1, keepdims=True) / total
        grad_score = (wide * (grad_prob - inner)).astype(BF)
        grad_query = (mm(grad_score, keys) * (coef_ref[...] / total)).astype(BF)
        glow_ref[...] += mm(grad_query, up, NT)
        out_ref[:, :, h, :, pl.ds(256, HEAD)] = mm(low_ref[...], grad_query, TN).astype(BF).reshape(2, NX, 8, HEAD)
        return carry

    lax.fori_loop(0, HEADS, head_step, 0)
    grad_low = glow_ref[...].astype(BF)

    def down_step(f, carry):
        cols = pl.ds(pl.multiple_of(f * 256, 256), 256)
        out_ref[:, :, f, :, pl.ds(0, 256)] = mm(grad_low, normed[:, cols], TN).astype(BF).reshape(2, NX, 8, 256)
        return carry

    lax.fori_loop(0, FS, down_step, 0)


def local_math(lengths, win, dp_fs, seq, hidden, frozen, grad, kv, par):
    smem = pl.BlockSpec(memory_space=pltpu.SMEM)
    vmem = pl.BlockSpec(memory_space=pltpu.VMEM)
    return pl.pallas_call(
        math_kernel,
        out_shape=jax.ShapeDtypeStruct((2, NX, FS, 8, PCOLS), BF),
        in_specs=[smem, smem, smem] + [vmem] * 6,
        out_specs=vmem,
        scratch_shapes=[
            pltpu.VMEM((ROWS, WIDTH), BF),
            pltpu.VMEM((ROWS, RANK), BF),
            pltpu.VMEM((ROWS, RANK), F32),
            pltpu.VMEM((ROWS, 1), F32),
            pltpu.VMEM((ROWS, 1), F32),
            pltpu.VMEM((ROWS, RANK), F32),
        ],
        compiler_params=pltpu.CompilerParams(vmem_limit_bytes=48 * 1024 * 1024),
        name="local_math",
    )(lengths, win, dp_fs, seq, hidden, frozen, grad, kv, par)


def reduce_kernel(
    part_ref, down_out, up_out,
    r0, s0, r1, s1, r2, s2, r3, s4,
    sem0s, sem0r, sem1s, sem1r, sem2s, sem2r, sem3s, sem3r, sem4s, sem4r,
):
    x, yh, core, yl, z = place()
    y = yh * 2 + yl
    other = 1 - core
    twin = dev(x, yh, other, yl, z)
    xs = [dev(lax.rem(x + d, NX), yh, core, yl, z) for d in range(1, NX)]
    xo = [dev(lax.rem(x + d, NX), yh, other, yl, z) for d in range(1, NX)]
    ys = [lax.rem(y + d, 8) for d in range(1, 8)]
    zs = [lax.rem(z + d, NZ) for d in range(1, NZ)]
    ydev = [dev(x, n // 2, core, lax.rem(n, 2), z) for n in ys]
    zdev = [dev(x, yh, core, yl, n) for n in zs]
    greet([twin] + xs + xo + ydev + zdev)

    copies = []
    for i in range(NX):
        copies.append(send(part_ref.at[other, i], r0.at[i], sem0s.at[i], sem0r.at[i], twin))
    steps = []
    for i in range(NX):
        copies[i].wait_recv()
        s0[i] = (part_ref[core, i].astype(F32) + r0[i].astype(F32)).astype(BF)
    for d in range(1, NX):
        steps.append(send(s0.at[lax.rem(x + d, NX)], r1.at[d - 1], sem1s.at[d - 1], sem1r.at[d - 1], xs[d - 1]))
    for copy in steps:
        copy.wait_recv()
    total = s0[x].astype(F32)
    for d in range(1, NX):
        total = total + r1[d - 1].astype(F32)
    s1[...] = total.astype(BF).reshape(2, NZ, 8, PCOLS)
    copies += steps
    steps = []
    for d in range(1, NZ):
        steps.append(send(s1.at[:, zs[d - 1]], r2.at[d - 1], sem2s.at[d - 1], sem2r.at[d - 1], zdev[d - 1]))
    total = s1[:, z].astype(F32)
    for d in range(1, NZ):
        steps[d - 1].wait_recv()
        total = total + r2[d - 1].astype(F32)
    s2[...] = total.astype(BF)
    copies += steps
    steps = []
    for d in range(1, 8):
        steps.append(send(s2.at[lax.rem(ys[d - 1], 2)], r3.at[y], sem3s.at[d - 1], sem3r.at[d - 1], ydev[d - 1]))
    r3[y] = s2[yl]
    for copy in steps:
        copy.wait_recv()
    total = r3[0].astype(F32)
    for j in range(1, 8):
        total = total + r3[j].astype(F32)
    copies += steps
    s4[core, x] = total
    steps = []
    for d, where in enumerate([twin] + xs + xo):
        steps.append(send(s4.at[core, x], s4.at[core, x], sem4s.at[d], sem4r.at[d], where))
    for copy in steps:
        copy.wait_recv()
    whole = s4[...].reshape(RANK, PCOLS)
    down_out[...] = whole[:, 0:256]
    up_out[...] = whole[:, 256:384]
    for copy in copies + steps:
        copy.wait_send()


def reduce(part):
    vmem = pl.BlockSpec(memory_space=pltpu.VMEM)
    dma = pltpu.SemaphoreType.DMA
    return pl.pallas_call(
        reduce_kernel,
        out_shape=(jax.ShapeDtypeStruct((RANK, 256), F32), jax.ShapeDtypeStruct((RANK, HEAD), F32)),
        in_specs=[vmem],
        out_specs=(vmem, vmem),
        scratch_shapes=[
            pltpu.VMEM((NX, FS, 8, PCOLS), BF),
            pltpu.VMEM((NX, FS, 8, PCOLS), BF),
            pltpu.VMEM((NX - 1, FS, 8, PCOLS), BF),
            pltpu.VMEM((2, NZ, 8, PCOLS), BF),
            pltpu.VMEM((NZ - 1, 2, 8, PCOLS), BF),
            pltpu.VMEM((2, 8, PCOLS), BF),
            pltpu.VMEM((8, 8, PCOLS), BF),
            pltpu.VMEM((2, NX, 8, PCOLS), F32),
            dma((NX,)), dma((NX,)), dma((3,)), dma((3,)), dma((7,)), dma((7,)), dma((7,)), dma((7,)), dma((7,)), dma((7,)),
        ],
        compiler_params=pltpu.CompilerParams(collective_id=1, has_side_effects=True),
        name="reduce",
    )(part)


def body(
    hidden,
    frozen_query_rows,
    output_gradient,
    token_log_ratio,
    lengths,
    response_win_probability,
    cached_prompt_keys,
    cached_prompt_values,
    adapter_down_factor,
    adapter_up_factor,
    attention_norm_gain,
):
    gain8 = jnp.broadcast_to(jnp.pad(attention_norm_gain, (0, PCOLS - 256))[None, :], (8, PCOLS))
    seq, kv, par = gather(
        lengths,
        token_log_ratio.reshape(RESP, 64),
        cached_prompt_keys,
        cached_prompt_values,
        adapter_down_factor.T,
        adapter_up_factor,
        gain8,
    )
    dp_fs = jnp.stack([lax.axis_index("dp"), lax.axis_index("fsdp")]).astype(jnp.int32)
    part = local_math(
        lengths,
        response_win_probability,
        dp_fs,
        seq,
        hidden.reshape(ROWS, WIDTH),
        frozen_query_rows.reshape(ROWS, HEADS * HEAD),
        output_gradient.reshape(ROWS, HEADS * HEAD),
        kv,
        par,
    )
    grad_down_t, grad_up = reduce(part)
    return grad_down_t.T, grad_up, seq[0:RESP, 0]


def solution(mesh):
    in_specs = (
        P(None, "dp", "fsdp", None),
        P(None, "dp", "fsdp", None),
        P(None, "dp", "fsdp", None),
        P(None, "dp", "fsdp"),
        P(),
        P(),
        P("fsdp", None),
        P("fsdp", None),
        P("fsdp", None),
        P(None, "fsdp"),
        P("fsdp"),
    )
    out_specs = (P("fsdp", None), P(None, "fsdp"), P())
    return jax.shard_map(body, mesh=mesh, in_specs=in_specs, out_specs=out_specs, check_vma=False)
```

time: 575 us -> 133 us (0.23)
  waiting for transfers between devices: 292 us -> 0 us
  blocking collectives: 183 us -> 0 us
  Pallas kernels: 0 us -> 118 us
  matrix products: 45.8 us -> 0 us
  between operations: 14.1 us -> 0.69 us
  other arithmetic: 13.1 us -> 0.08 us
  local copies, waits for them, and re-layouts: 25.3 us -> 12.8 us
    psum x1 -> x0, waiting for transfers between devices: 290 us -> none  [body(): down_sum, up_sum = lax.psum((down_term, up_term), ('dp', 'fsdp'))]
    pallas_call x0 -> x3, Pallas kernels: none -> 118 us  [the longest x1 60.5 us: gather(): pl.pallas_call(gather_kernel, out_shape=(jax.ShapeDtypeStruct((8, 128), F...]
    psum x1 -> x0, blocking collectives: 107 us -> none  [body(): seq_ratio = lax.psum(partial_value, ('dp', 'fsdp'))]
    all_gather x3 -> x0, blocking collectives: 76.1 us -> none  [the longest x1 27.2 us: body(): lax.all_gather(adapter_down_factor, 'fsdp', axis=0, tiled=True)]
    dot_general x16 -> x0, matrix products: 45.8 us -> none  [the longest x4 19.2 us: attend(): jnp.einsum('nhj,jd->nhd', grad_score, head_key, preferred_element_type=jn...]
    reduce_sum x10 -> x0, other arithmetic: 9.91 us -> none  [the longest x4 3.92 us: attend(): row_total = jnp.sum(exponent, axis=2, keepdims=True)]
    reshape x4 -> x0, local copies, waits for them, and re-layouts: 5.92 us -> none  [attend(): cotangent[:, head_start:head_stop]]
  transfers between devices with their start and end apart: 3 -> 0, of which waited for: 1 -> 0; matrix products, arithmetic and copies ran while one was open for 3% -> 0% of each run, Pallas kernels for 0% -> 0%
where the time goes in v1:
time: 133 us; the launch traced here: 132 us
  Pallas kernels  118 us (89%)
  local copies, waits for them, and re-layouts  12.8 us (10%)
    pallas_call x1, Pallas kernels, gather(): pl.pallas_call(gather_kernel, out_shape=(jax.ShapeDtypeStruct((8, 128), F...  60.5 us
    pallas_call x1, Pallas kernels, reduce(): pl.pallas_call(reduce_kernel, out_shape=(jax.ShapeDtypeStruct((RANK, 256)...  30.5 us
    pallas_call x1, Pallas kernels, local_math(): pl.pallas_call(math_kernel, out_shape=jax.ShapeDtypeStruct((2, NX, FS, 8,...  27.4 us
    unnamed x20, local copies, waits for them, and re-layouts  10.9 us

profile of v1, /device:TPU:1, one launch (start us, length us, event | category | flops | bytes accessed | tf_op | source)
XLA Modules:
  0.0 132.0 jit_solution(13268079599657835924)
XLA Ops:
  0.6 0.1 pad_add_fusion.dp_ref
  0.7 0.7 pad.4
  1.4 0.6 broadcast_in_dim.2.gain_ref
  2.0 60.5 %gather.1 = (f32[8,128]{1,0:T(8,128)}, bf16[2,4,16,64,128]{4,3,2,1,0:T(8,128)(2,1)}, bf16[2,16,40,384]{3,2,1,0:T(8,128)(2,1)}) custom-call(s32[4]{0:T(128)} %lengths_ref.3, f32[4,64]{1,0:T(4,128)} %bitcast.13, bf16[64,512]{1,0:T(8,128)(2,1)} %k_ref.1, bf16[64,512]{1,0:T(8,128)(2,1)} %v_ref.1, bf16[64,256]{1,0:T(8,128)(2,1)} %bitcast.12, ...), custom_call_target="tpu_custom_call" | custom-call | tf_op jit(solution)/shard_map/gather/pallas_call | solution.py:200
  62.4 0.0 copy-start.1
  62.4 1.6 %copy-done.1 = bf16[4,64,1,4096]{3,1,2,0:T(8,128)(2,1)S(1)} copy-done((bf16[4,64,1,4096]{3,1,2,0:T(8,128)(2,1)S(1)}, bf16[4,64,1,4096]{3,1,2,0:T(8,128)(2,1)}, u32[]{:S(2)}) %copy-start.1) | copy-done | bytes 2097176
  64.0 0.0 copy-start.2
  64.0 1.2 copy-done.2
  65.3 0.0 copy-start.3
  65.3 1.2 copy-done.3
  66.5 0.0 copy-start.4
  66.5 1.2 copy-done.4
  67.7 0.0 copy-start.5
  67.7 0.7 copy-done.5
  68.3 0.0 copy-start.7
  68.3 0.7 copy-done.7
  69.0 0.0 copy-start.8
  69.0 0.7 copy-done.8
  69.7 0.0 copy-start.6
  69.7 27.4 %local_math.1.part_ref = bf16[2,4,16,8,384]{4,3,2,1,0:T(8,128)(2,1)S(1)} custom-call(s32[4]{0:T(128)S(1)} %copy-done.7, f32[4]{0:T(128)S(1)} %copy-done.8, s32[2]{0:T(128)S(1)} %pad_add_fusion.dp_ref, f32[8,128]{1,0:T(8,128)S(1)} %copy-done.5, bf16[256,4096]{1,0:T(8,128)(2,1)S(1)} %bitcast.8, bf16[256,2048]{1,0:T(8,128)(2,1)S(1)} %bitcast.9, ...), custom_call_target="tpu_custom_call" | custom-call | tf_op jit(solution)/shard_map/local_math/pallas_call | solution.py:311
  97.1 0.0 copy-start
  97.1 0.9 copy-done
  98.0 30.5 %reduce.3 = (f32[64,256]{1,0:T(8,128)}, f32[64,128]{1,0:T(8,128)}) custom-call(bf16[2,4,16,8,384]{4,3,2,1,0:T(8,128)(2,1)} %copy-done), custom_call_target="tpu_custom_call" | custom-call | tf_op jit(solution)/shard_map/reduce/pallas_call | solution.py:397
  128.5 0.0 copy-done.6
  128.5 0.6 slice_reduce_fusion
  129.1 1.5 %copy.16 = f32[256,64]{0,1:T(8,128)} copy(f32[256,64]{0,1:T(8,128)} %bitcast.11) | data formatting | bytes 131072
  130.6 1.4 %copy.17 = f32[64,128]{1,0:T(8,128)} copy(f32[64,128]{1,0:T(8,128)} %get-tuple-element.17) | data formatting | bytes 65536
Async XLA Ops:
  62.4 1.6 %copy-start.1 = (bf16[4,64,1,4096]{3,1,2,0:T(8,128)(2,1)S(1)}, bf16[4,64,1,4096]{3,1,2,0:T(8,128)(2,1)}, u32[]{:S(2)}) copy-start(bf16[4,64,1,4096]{3,1,2,0:T(8,128)(2,1)} %param.11) | copy-start | bytes 6291460
  64.0 1.2 copy-start.2
  65.3 1.2 copy-start.3
  66.5 1.2 copy-start.4
  67.7 0.7 copy-start.5
  68.3 0.7 copy-start.7
  69.0 0.7 copy-start.8
  69.7 58.8 %copy-start.6 = (f32[8,128]{1,0:T(8,128)S(1)}, f32[8,128]{1,0:T(8,128)}, u32[]{:S(2)}) copy-start(f32[8,128]{1,0:T(8,128)} %get-tuple-element.8.seq_ref) | copy-start | bytes 12292
  97.1 0.9 copy-start

commit v2 on v0

v2 whole, which is shorter than its diff:
```python
import math

import jax
import jax.numpy as jnp
from jax import lax
from jax.experimental import pallas as pl
from jax.experimental.pallas import tpu as pltpu
from jax.sharding import PartitionSpec as P

MESH = pl.DeviceIdType.MESH
HEAD = 128
HEADS = 16
GROUPS = 4
RANK = 64
WIDTH = 4096
PROMPT = 1024
RESP = 4
ROWS = 256
FS = 16
NZ, NX, NYH = 8, 4, 4
PCOLS = 384
EPS = 1e-05
BF, F32 = jnp.bfloat16, jnp.float32


def place():
    dp = lax.axis_index("dp")
    fs = lax.axis_index("fsdp")
    core = lax.rem(dp, 2)
    yh = lax.rem(dp // 2, NYH)
    x = dp // (2 * NYH)
    z = lax.rem(fs, NZ)
    yl = fs // NZ
    return x, yh, core, yl, z


def dev(x, yh, core, yl, z):
    return ((x * NYH + yh) * 2 + core, yl * NZ + z)


def send(src, dst, ssem, rsem, where):
    copy = pltpu.make_async_remote_copy(
        src_ref=src, dst_ref=dst, send_sem=ssem, recv_sem=rsem, device_id=where, device_id_type=MESH
    )
    copy.start()
    return copy


def greet(peers):
    barrier = pltpu.get_barrier_semaphore()
    for where in peers:
        pl.semaphore_signal(barrier, inc=1, device_id=where, device_id_type=MESH)
    pl.semaphore_wait(barrier, len(peers))


NT = (((1,), (1,)), ((), ()))
TN = (((0,), (0,)), ((), ()))
PER = HEADS // GROUPS
SCALE = 1.0 / math.sqrt(HEAD)


def mm(a, b, dims=(((1,), (0,)), ((), ()))):
    return lax.dot_general(a, b, dims, preferred_element_type=F32)


def step_kernel(
    lengths_ref, win_ref, tlr_ref, k_ref, v_ref, down_ref, up_ref, gain_ref, hidden_hbm, frozen_hbm, grad_hbm,
    seq_out, down_out, up_out,
    kv, par, gains, hidden, frozen, grad, normed, low_ref, low32, inv_ref, coef_ref, glow_ref,
    tot1, tot2, part, r0, s0, r1, s1, r2, s2, r3, s4,
    load_sem, big_sem, as_sem, ar_sem, gs_sem, gr_sem, cs_sem, cr_sem, t1s, t1r, t2s, t2r,
    sem0s, sem0r, sem1s, sem1r, sem2s, sem2r, sem3s, sem3r, sem4s, sem4r,
):
    x, yh, core, yl, z = place()
    me = yl * NZ + z
    y = yh * 2 + yl
    spot = lax.axis_index("dp")
    other = 1 - core
    twin = dev(x, yh, other, yl, z)
    hops = [(d, e) for d in (0, 1, 7, 2, 6, 3, 5, 4) for e in (0, 1) if (d, e) != (0, 0)]
    fs_at = [(lax.rem(z + d, NZ), lax.rem(yl + e, 2)) for d, e in hops]
    fs_from = [(lax.rem(z + NZ - d, NZ), lax.rem(yl + e, 2)) for d, e in hops]
    fs_dev = [dev(x, yh, core, b, a) for a, b in fs_at]
    dp_dev = [(lax.rem(spot + d, 32), me) for d in range(1, 32)]
    xs = [dev(lax.rem(x + d, NX), yh, core, yl, z) for d in range(1, NX)]
    xo = [dev(lax.rem(x + d, NX), yh, other, yl, z) for d in range(1, NX)]
    ys = [lax.rem(y + d, 8) for d in range(1, 8)]
    zs = [lax.rem(z + d, NZ) for d in range(1, NZ)]
    y_dev = [dev(x, n // 2, core, lax.rem(n, 2), z) for n in ys]
    z_dev = [dev(x, yh, core, yl, n) for n in zs]
    across = [dev(x, lax.rem(yh + d, NYH), core, 1 - yl, z) for d in range(1, NYH)]

    barrier = pltpu.get_barrier_semaphore()
    greeted = fs_dev + dp_dev + across
    for where in greeted:
        pl.semaphore_signal(barrier, inc=1, device_id=where, device_id_type=MESH)

    rows = pl.ds(pl.multiple_of(core * 32, 32), 32)
    loads = [
        pltpu.make_async_copy(down_ref.at[rows, :], par.at[core, me, :, pl.ds(0, 256)], load_sem.at[0]),
        pltpu.make_async_copy(up_ref.at[rows, :], par.at[core, me, :, pl.ds(256, HEAD)], load_sem.at[1]),
        pltpu.make_async_copy(gain_ref, gains.at[me], load_sem.at[2]),
    ]
    for copy in loads:
        copy.start()
    for kind, src in ((0, k_ref), (1, v_ref)):

        @pl.when(core == kind)
        def _():
            for g in range(GROUPS):
                pltpu.make_async_copy(src.at[:, pl.ds(g * HEAD, HEAD)], kv.at[kind, g, me], load_sem.at[3 + g]).start()

    bigs = [
        pltpu.make_async_copy(hidden_hbm, hidden, big_sem.at[0]),
        pltpu.make_async_copy(frozen_hbm, frozen, big_sem.at[1]),
        pltpu.make_async_copy(grad_hbm, grad, big_sem.at[2]),
    ]
    for copy in bigs:
        copy.start()

    place_row = lax.broadcasted_iota(jnp.int32, (RESP, 64), 1)
    resp = lax.broadcasted_iota(jnp.int32, (RESP, 64), 0)
    position = (spot * 64 + place_row) * FS + me
    limit = jnp.full((RESP, 64), lengths_ref[0], jnp.int32)
    for r in range(1, RESP):
        limit = jnp.where(resp == r, lengths_ref[r], limit)
    mine = jnp.sum(jnp.where(position < limit, tlr_ref[...], 0.0), axis=1, keepdims=True)
    tot1[me] = jnp.concatenate([jnp.broadcast_to(mine, (RESP, 128)), jnp.zeros((8 - RESP, 128), F32)], axis=0)

    for copy in loads:
        copy.wait()
    for g in range(GROUPS):
        pltpu.make_async_copy(k_ref.at[:, pl.ds(g * HEAD, HEAD)], kv.at[core, g, me], load_sem.at[3 + g]).wait()
    pl.semaphore_wait(barrier, len(greeted))

    sent = []
    for i, where in enumerate(fs_dev):
        sent.append(send(gains.at[me], gains.at[me], gs_sem.at[i], gr_sem.at[i], where))
    for i, where in enumerate(fs_dev):
        sent.append(send(par.at[core, me], par.at[core, me], as_sem.at[GROUPS, i], ar_sem.at[GROUPS, i], where))
    for i, where in enumerate(fs_dev):
        sent.append(send(tot1.at[me], tot1.at[me], t1s.at[i], t1r.at[i], where))
    for g in range(GROUPS):
        for i, where in enumerate(fs_dev):
            sent.append(send(kv.at[core, g, me], kv.at[core, g, me], as_sem.at[g, i], ar_sem.at[g, i], where))

    def landed(ref, sem):
        pltpu.make_async_remote_copy(
            src_ref=ref, dst_ref=ref, send_sem=sem, recv_sem=sem, device_id=twin, device_id_type=MESH
        ).wait_recv()

    def origin(i):
        a, b = fs_from[i]
        return b * NZ + a

    bigs[0].wait()
    square = jnp.zeros((ROWS, 256), F32)
    for f in range(FS):
        block = hidden[:, pl.ds(f * 256, 256)].astype(F32)
        square = square + block * block
    inv_ref[...] = lax.rsqrt(jnp.sum(square, axis=1, keepdims=True) * (1.0 / WIDTH) + EPS)
    low32[...] = jnp.zeros_like(low32)
    for i in range(len(fs_dev)):
        landed(gains.at[origin(i)], gr_sem.at[i])

    def norm_step(f, carry):
        gain = gains[f].astype(F32)
        for half in range(2):
            cols = pl.ds(pl.multiple_of(f * 256 + half * 128, 128), 128)
            normed[:, cols] = (hidden[:, cols].astype(F32) * inv_ref[...] * gain[half : half + 1]).astype(BF)
        return carry

    lax.fori_loop(0, FS, norm_step, 0)

    for i in range(len(fs_dev)):
        landed(tot1.at[origin(i)], t1r.at[i])
    total = tot1[0]
    for j in range(1, FS):
        total = total + tot1[j]
    tot2[spot] = total
    for d in range(31):
        sent.append(send(tot2.at[spot], tot2.at[spot], t2s.at[d], t2r.at[d], dp_dev[d]))

    for i in range(len(fs_dev)):
        landed(par.at[core, origin(i)], ar_sem.at[GROUPS, i])
    swap = send(par.at[core], par.at[core], cs_sem.at[GROUPS], cr_sem.at[GROUPS], twin)
    sent.append(swap)
    for i in range(len(fs_dev)):
        landed(kv.at[core, 0, origin(i)], ar_sem.at[0, i])
    first = send(kv.at[core, 0], kv.at[core, 0], cs_sem.at[0], cr_sem.at[0], twin)
    landed(par.at[other], cr_sem.at[GROUPS])

    def low_step(f, carry):
        cols = pl.ds(pl.multiple_of(f * 256, 256), 256)
        low32[...] += mm(normed[:, cols], par[:, f, :, pl.ds(0, 256)].reshape(RANK, 256), NT)
        return carry

    lax.fori_loop(0, FS, low_step, 0)
    low_ref[...] = low32[...].astype(BF)
    glow_ref[...] = jnp.zeros_like(glow_ref)

    for d in range(31):
        landed(tot2.at[lax.rem(spot + 31 - d, 32)], t2r.at[d])
    total = tot2[0]
    for j in range(1, 32):
        total = total + tot2[j]
    seq_out[...] = total
    row = lax.broadcasted_iota(jnp.int32, (64, 1), 0)
    position = (spot * 64 + row) * FS + me
    for r in range(RESP):
        weight = 2.0 * (total[r : r + 1, 0:1] - (win_ref[r] - 0.5)) / RESP
        coef_ref[pl.ds(r * 64, 64), :] = jnp.where(position < lengths_ref[r], jnp.broadcast_to(weight, (64, 1)), 0.0) * SCALE
    bigs[1].wait()
    bigs[2].wait()

    def group_step(g, carry):
        @pl.when(g < GROUPS - 1)
        def _():
            for i in range(len(fs_dev)):
                landed(kv.at[core, g + 1, origin(i)], ar_sem.at[g + 1, i])
            send(kv.at[core, g + 1], kv.at[core, g + 1], cs_sem.at[g + 1], cr_sem.at[g + 1], twin)

        landed(kv.at[other, g], cr_sem.at[g])
        ups, queries, grads = [], [], []
        for a in range(PER):
            h = g * PER + a
            cols = pl.ds(pl.multiple_of(h * HEAD, HEAD), HEAD)
            ups.append(par[:, h, :, pl.ds(256, HEAD)].reshape(RANK, HEAD))
            queries.append((frozen[:, cols].astype(F32) + mm(low_ref[...], ups[a])).astype(BF))
            grads.append(grad[:, cols])
        keys = kv[0, g].reshape(PROMPT, HEAD)
        values = kv[1, g].reshape(PROMPT, HEAD)
        scores = mm(jnp.concatenate(queries, axis=0), keys, NT)
        top = jnp.max(scores, axis=1, keepdims=True)
        expo = jnp.exp2((scores - top) * (SCALE * math.log2(math.e)))
        row_total = jnp.sum(expo, axis=1, keepdims=True)
        weights = expo.astype(BF)
        grad_prob = mm(jnp.concatenate(grads, axis=0), values, NT)
        wide = weights.astype(F32)
        inner = jnp.sum(wide * grad_prob, axis=1, keepdims=True) / row_total
        grad_score = (wide * (grad_prob - inner)).astype(BF)
        coef = jnp.concatenate([coef_ref[...]] * PER, axis=0)
        grad_query = (mm(grad_score, keys) * (coef / row_total)).astype(BF)
        for a in range(PER):
            h = g * PER + a
            block = grad_query[a * ROWS : (a + 1) * ROWS]
            glow_ref[...] += mm(block, ups[a], NT)
            part[:, :, h, :, pl.ds(256, HEAD)] = mm(low_ref[...], block, TN).astype(BF).reshape(2, NX, 8, HEAD)
        return carry

    lax.fori_loop(0, GROUPS, group_step, 0)
    grad_low = glow_ref[...].astype(BF)

    pieces = 4
    size = FS // pieces
    swaps, steps = [], []

    def pass_x(p):
        blocks = pl.ds(p * size, size)
        swaps[p].wait_recv()
        s0[:, blocks] = (part[core, :, blocks].astype(F32) + r0[:, blocks].astype(F32)).astype(BF)
        for d in range(1, NX):
            steps.append(send(s0.at[lax.rem(x + d, NX), blocks], r1.at[d - 1, blocks], sem1s.at[p, d - 1], sem1r.at[p, d - 1], xs[d - 1]))

    for p in range(pieces):
        for f in range(p * size, (p + 1) * size):
            part[:, :, f, :, pl.ds(0, 256)] = mm(grad_low, normed[:, pl.ds(f * 256, 256)], TN).astype(BF).reshape(2, NX, 8, 256)
        blocks = pl.ds(p * size, size)
        swaps.append(send(part.at[other, :, blocks], r0.at[:, blocks], sem0s.at[p], sem0r.at[p], twin))
        if p:
            pass_x(p - 1)
    pass_x(pieces - 1)
    for copy in steps:
        copy.wait_recv()
    sum_x = s0[x].astype(F32)
    for d in range(1, NX):
        sum_x = sum_x + r1[d - 1].astype(F32)
    s1[...] = sum_x.astype(BF).reshape(2, NZ, 8, PCOLS)
    sent += swaps + steps
    steps = []
    for d in range(1, NZ):
        steps.append(send(s1.at[:, zs[d - 1]], r2.at[d - 1], sem2s.at[d - 1], sem2r.at[d - 1], z_dev[d - 1]))
    sum_z = s1[:, z].astype(F32)
    for d in range(1, NZ):
        steps[d - 1].wait_recv()
        sum_z = sum_z + r2[d - 1].astype(F32)
    s2[...] = sum_z.astype(BF)
    sent += steps
    steps = []
    for d in range(1, 8):
        steps.append(send(s2.at[lax.rem(ys[d - 1], 2)], r3.at[y], sem3s.at[d - 1], sem3r.at[d - 1], y_dev[d - 1]))
    r3[y] = s2[yl]
    for copy in steps:
        copy.wait_recv()
    sum_y = r3[0].astype(F32)
    for j in range(1, 8):
        sum_y = sum_y + r3[j].astype(F32)
    sent += steps
    s4[core, x] = sum_y
    steps = []
    for d, where in enumerate([twin] + xs + xo):
        steps.append(send(s4.at[core, x], s4.at[core, x], sem4s.at[d], sem4r.at[d], where))
    for copy in steps:
        copy.wait_recv()
    whole = s4[...].reshape(RANK, PCOLS)
    down_out[...] = whole[:, 0:256]
    up_out[...] = whole[:, 256:384]
    for copy in sent + steps:
        copy.wait_send()
    for g in range(GROUPS):
        pltpu.make_async_remote_copy(
            src_ref=kv.at[core, g], dst_ref=kv.at[core, g], send_sem=cs_sem.at[g], recv_sem=cr_sem.at[g],
            device_id=twin, device_id_type=MESH,
        ).wait_send()


def step(*args):
    any_ = pl.BlockSpec(memory_space=pl.ANY)
    vmem = pl.BlockSpec(memory_space=pltpu.VMEM)
    smem = pl.BlockSpec(memory_space=pltpu.SMEM)
    dma = pltpu.SemaphoreType.DMA
    wide = HEADS * HEAD
    return pl.pallas_call(
        step_kernel,
        out_shape=(
            jax.ShapeDtypeStruct((8, 128), F32),
            jax.ShapeDtypeStruct((RANK, 256), F32),
            jax.ShapeDtypeStruct((RANK, HEAD), F32),
        ),
        in_specs=[smem, smem, vmem] + [any_] * 8,
        out_specs=(vmem, vmem, vmem),
        scratch_shapes=[
            pltpu.VMEM((2, GROUPS, FS, 64, HEAD), BF),
            pltpu.VMEM((2, FS, 32, PCOLS), BF),
            pltpu.VMEM((FS, 2, 128), BF),
            pltpu.VMEM((ROWS, WIDTH), BF),
            pltpu.VMEM((ROWS, wide), BF),
            pltpu.VMEM((ROWS, wide), BF),
            pltpu.VMEM((ROWS, WIDTH), BF),
            pltpu.VMEM((ROWS, RANK), BF),
            pltpu.VMEM((ROWS, RANK), F32),
            pltpu.VMEM((ROWS, 1), F32),
            pltpu.VMEM((ROWS, 1), F32),
            pltpu.VMEM((ROWS, RANK), F32),
            pltpu.VMEM((FS, 8, 128), F32),
            pltpu.VMEM((32, 8, 128), F32),
            pltpu.VMEM((2, NX, FS, 8, PCOLS), BF),
            pltpu.VMEM((NX, FS, 8, PCOLS), BF),
            pltpu.VMEM((NX, FS, 8, PCOLS), BF),
            pltpu.VMEM((NX - 1, FS, 8, PCOLS), BF),
            pltpu.VMEM((2, NZ, 8, PCOLS), BF),
            pltpu.VMEM((NZ - 1, 2, 8, PCOLS), BF),
            pltpu.VMEM((2, 8, PCOLS), BF),
            pltpu.VMEM((8, 8, PCOLS), BF),
            pltpu.VMEM((2, NX, 8, PCOLS), F32),
            dma((7,)), dma((3,)),
            dma((GROUPS + 1, 15)), dma((GROUPS + 1, 15)),
            dma((15,)), dma((15,)),
            dma((GROUPS + 1,)), dma((GROUPS + 1,)),
            dma((15,)), dma((15,)), dma((31,)), dma((31,)),
            dma((4,)), dma((4,)), dma((4, 3)), dma((4, 3)),
            dma((7,)), dma((7,)), dma((7,)), dma((7,)), dma((7,)), dma((7,)),
        ],
        compiler_params=pltpu.CompilerParams(collective_id=0, has_side_effects=True, vmem_limit_bytes=60 * 1024 * 1024),
        name="step",
    )(*args)


def body(
    hidden,
    frozen_query_rows,
    output_gradient,
    token_log_ratio,
    lengths,
    response_win_probability,
    cached_prompt_keys,
    cached_prompt_values,
    adapter_down_factor,
    adapter_up_factor,
    attention_norm_gain,
):
    seq, grad_down_t, grad_up = step(
        lengths,
        response_win_probability,
        token_log_ratio.reshape(RESP, 64),
        cached_prompt_keys,
        cached_prompt_values,
        adapter_down_factor.T,
        adapter_up_factor,
        attention_norm_gain.reshape(2, 128),
        hidden.reshape(ROWS, WIDTH),
        frozen_query_rows.reshape(ROWS, HEADS * HEAD),
        output_gradient.reshape(ROWS, HEADS * HEAD),
    )
    return grad_down_t.T, grad_up, seq[0:RESP, 0]


def solution(mesh):
    in_specs = (
        P(None, "dp", "fsdp", None),
        P(None, "dp", "fsdp", None),
        P(None, "dp", "fsdp", None),
        P(None, "dp", "fsdp"),
        P(),
        P(),
        P("fsdp", None),
        P("fsdp", None),
        P("fsdp", None),
        P(None, "fsdp"),
        P("fsdp"),
    )
    out_specs = (P("fsdp", None), P(None, "fsdp"), P())
    return jax.shard_map(body, mesh=mesh, in_specs=in_specs, out_specs=out_specs, check_vma=False)
```

time: 575 us -> 94.8 us (0.16)
  waiting for transfers between devices: 292 us -> 0 us
  blocking collectives: 183 us -> 0 us
  Pallas kernels: 0 us -> 89.7 us
  matrix products: 45.8 us -> 0 us
  local copies, waits for them, and re-layouts: 25.3 us -> 4.16 us
  between operations: 14.1 us -> 0.64 us
  other arithmetic: 13.1 us -> 0 us
    psum x1 -> x0, waiting for transfers between devices: 290 us -> none  [body(): down_sum, up_sum = lax.psum((down_term, up_term), ('dp', 'fsdp'))]
    psum x1 -> x0, blocking collectives: 107 us -> none  [body(): seq_ratio = lax.psum(partial_value, ('dp', 'fsdp'))]
    pallas_call x0 -> x1, Pallas kernels: none -> 89.7 us  [step(): pl.pallas_call(step_kernel, out_shape=(jax.ShapeDtypeStruct((8, 128), F32...]
    all_gather x3 -> x0, blocking collectives: 76.1 us -> none  [the longest x1 27.2 us: body(): lax.all_gather(adapter_down_factor, 'fsdp', axis=0, tiled=True)]
    dot_general x16 -> x0, matrix products: 45.8 us -> none  [the longest x4 19.2 us: attend(): jnp.einsum('nhj,jd->nhd', grad_score, head_key, preferred_element_type=jn...]
    reduce_sum x10 -> x0, other arithmetic: 9.91 us -> none  [the longest x4 3.92 us: attend(): row_total = jnp.sum(exponent, axis=2, keepdims=True)]
    unnamed x67 -> x2, local copies, waits for them, and re-layouts: 11 us -> 2.85 us
    reshape x4 -> x0, local copies, waits for them, and re-layouts: 5.92 us -> none  [attend(): cotangent[:, head_start:head_stop]]
  transfers between devices with their start and end apart: 3 -> 0, of which waited for: 1 -> 0; matrix products, arithmetic and copies ran while one was open for 3% -> 0% of each run, Pallas kernels for 0% -> 0%
where the time goes in v2:
time: 94.8 us; the launch traced here: 94.5 us
  Pallas kernels  89.7 us (95%)
  local copies, waits for them, and re-layouts  4.16 us (4%)
    pallas_call x1, Pallas kernels, step(): pl.pallas_call(step_kernel, out_shape=(jax.ShapeDtypeStruct((8, 128), F32...  89.7 us
    unnamed x2, local copies, waits for them, and re-layouts  2.85 us

profile of v2, /device:TPU:1, one launch (start us, length us, event | category | flops | bytes accessed | tf_op | source)
XLA Modules:
  0.0 94.5 jit_solution(4053750802267270775)
XLA Ops:
  0.6 89.7 %step.1 = (f32[8,128]{1,0:T(8,128)}, f32[64,256]{1,0:T(8,128)}, f32[64,128]{1,0:T(8,128)}) custom-call(s32[4]{0:T(128)} %lengths_ref.1, f32[4]{0:T(128)} %win_ref.1, f32[4,64]{1,0:T(4,128)} %bitcast.12, bf16[64,512]{1,0:T(8,128)(2,1)} %k_ref.1, bf16[64,512]{1,0:T(8,128)(2,1)} %v_ref.1, bf16[64,256]{1,0:T(8,128)(2,1)} %bitcast.11, bf16[64,128]{1,0:T(8,128)(2,1)} %up_ref.1, ...), custom_call_target="tpu_custom_call" | custom-call | tf_op jit(solution)/shard_map/step/pallas_call | solution.py:323
  90.4 1.3 %slice_reduce_fusion = f32[4]{0:T(128)} fusion(f32[8,128]{1,0:T(8,128)} %get-tuple-element.8), kind=kLoop, calls=%fused_computation | loop fusion | bytes 32 | tf_op jit(solution)/shard_map/slice | solution.py:395
  91.7 1.5 %copy.16 = f32[256,64]{0,1:T(8,128)} copy(f32[256,64]{0,1:T(8,128)} %bitcast.10) | data formatting | bytes 131072
  93.2 1.4 %copy.17 = f32[64,128]{1,0:T(8,128)} copy(f32[64,128]{1,0:T(8,128)} %get-tuple-element.13) | data formatting | bytes 65536

commit v3 on v2

--- a/solution.py
+++ b/solution.py
@@ -68,7 +68,7 @@
     seq_out, down_out, up_out,
     kv, par, gains, hidden, frozen, grad, normed, low_ref, low32, inv_ref, coef_ref, glow_ref,
     tot1, tot2, part, r0, s0, r1, s1, r2, s2, r3, s4,
-    load_sem, big_sem, as_sem, ar_sem, gs_sem, gr_sem, cs_sem, cr_sem, t1s, t1r, t2s, t2r,
+    load_sem, big_sem, as_sem, ar_sem, fs_sem, fr_sem, gs_sem, gr_sem, cs_sem, cr_sem, t1s, t1r, t2s, t2r,
     sem0s, sem0r, sem1s, sem1r, sem2s, sem2r, sem3s, sem3r, sem4s, sem4r,
 ):
     x, yh, core, yl, z = place()
@@ -86,8 +86,11 @@
     xo = [dev(lax.rem(x + d, NX), yh, other, yl, z) for d in range(1, NX)]
     ys = [lax.rem(y + d, 8) for d in range(1, 8)]
     zs = [lax.rem(z + d, NZ) for d in range(1, NZ)]
+    flip = dev(x, yh, core, 1 - yl, z)
+    z_hops = (1, 7, 2, 6, 3, 5, 4)
     y_dev = [dev(x, n // 2, core, lax.rem(n, 2), z) for n in ys]
     z_dev = [dev(x, yh, core, yl, n) for n in zs]
+    z_to = lambda d: dev(x, yh, core, yl, lax.rem(z + d, NZ))
     across = [dev(x, lax.rem(yh + d, NYH), core, 1 - yl, z) for d in range(1, NYH)]
 
     barrier = pltpu.get_barrier_semaphore()
@@ -136,13 +139,13 @@
     sent = []
     for i, where in enumerate(fs_dev):
         sent.append(send(gains.at[me], gains.at[me], gs_sem.at[i], gr_sem.at[i], where))
-    for i, where in enumerate(fs_dev):
-        sent.append(send(par.at[core, me], par.at[core, me], as_sem.at[GROUPS, i], ar_sem.at[GROUPS, i], where))
+    for i, d in enumerate(z_hops):
+        sent.append(send(par.at[core, me], par.at[core, me], as_sem.at[GROUPS, i], ar_sem.at[GROUPS, i], z_to(d)))
     for i, where in enumerate(fs_dev):
         sent.append(send(tot1.at[me], tot1.at[me], t1s.at[i], t1r.at[i], where))
     for g in range(GROUPS):
-        for i, where in enumerate(fs_dev):
-            sent.append(send(kv.at[core, g, me], kv.at[core, g, me], as_sem.at[g, i], ar_sem.at[g, i], where))
+        for i, d in enumerate(z_hops):
+            sent.append(send(kv.at[core, g, me], kv.at[core, g, me], as_sem.at[g, i], ar_sem.at[g, i], z_to(d)))
 
     def landed(ref, sem):
         pltpu.make_async_remote_copy(
@@ -152,6 +155,41 @@
     def origin(i):
         a, b = fs_from[i]
         return b * NZ + a
+
+    def plane(kind, chunk, b):
+        shards = pl.ds(pl.multiple_of(b * NZ, NZ), NZ)
+        return par.at[kind, shards] if chunk is None else kv.at[kind, chunk, shards]
+
+    def slot(chunk):
+        return GROUPS if chunk is None else chunk
+
+    def pass_flip(chunk):
+        at = slot(chunk)
+        for i, d in enumerate(z_hops):
+            shard = yl * NZ + lax.rem(z + NZ - d, NZ)
+            landed(par.at[core, shard] if chunk is None else kv.at[core, chunk, shard], ar_sem.at[at, i])
+        ref = plane(core, chunk, yl)
+        send(ref, ref, fs_sem.at[at], fr_sem.at[at], flip)
+        send(ref, ref, cs_sem.at[0, at], cr_sem.at[0, at], twin)
+
+    def pass_twin(chunk):
+        at = slot(chunk)
+        ref = plane(core, chunk, 1 - yl)
+        landed(ref, fr_sem.at[at])
+        send(ref, ref, cs_sem.at[1, at], cr_sem.at[1, at], twin)
+
+    def complete(chunk):
+        at = slot(chunk)
+        landed(plane(other, chunk, yl), cr_sem.at[0, at])
+        landed(plane(other, chunk, 1 - yl), cr_sem.at[1, at])
+
+    def left(chunk):
+        at = slot(chunk)
+        for sem, b in ((fs_sem.at[at], yl), (cs_sem.at[0, at], yl), (cs_sem.at[1, at], 1 - yl)):
+            ref = plane(core, chunk, b)
+            pltpu.make_async_remote_copy(
+                src_ref=ref, dst_ref=ref, send_sem=sem, recv_sem=sem, device_id=twin, device_id_type=MESH
+            ).wait_send()
 
     bigs[0].wait()
     square = jnp.zeros((ROWS, 256), F32)
@@ -172,6 +210,7 @@
 
     lax.fori_loop(0, FS, norm_step, 0)
 
+    pass_flip(None)
     for i in range(len(fs_dev)):
         landed(tot1.at[origin(i)], t1r.at[i])
     total = tot1[0]
@@ -180,15 +219,9 @@
     tot2[spot] = total
     for d in range(31):
         sent.append(send(tot2.at[spot], tot2.at[spot], t2s.at[d], t2r.at[d], dp_dev[d]))
-
-    for i in range(len(fs_dev)):
-        landed(par.at[core, origin(i)], ar_sem.at[GROUPS, i])
-    swap = send(par.at[core], par.at[core], cs_sem.at[GROUPS], cr_sem.at[GROUPS], twin)
-    sent.append(swap)
-    for i in range(len(fs_dev)):
-        landed(kv.at[core, 0, origin(i)], ar_sem.at[0, i])
-    first = send(kv.at[core, 0], kv.at[core, 0], cs_sem.at[0], cr_sem.at[0], twin)
-    landed(par.at[other], cr_sem.at[GROUPS])
+    pass_twin(None)
+    pass_flip(0)
+    complete(None)
 
     def low_step(f, carry):
         cols = pl.ds(pl.multiple_of(f * 256, 256), 256)
@@ -198,6 +231,8 @@
     lax.fori_loop(0, FS, low_step, 0)
     low_ref[...] = low32[...].astype(BF)
     glow_ref[...] = jnp.zeros_like(glow_ref)
+    pass_twin(0)
+    pass_flip(1)
 
     for d in range(31):
         landed(tot2.at[lax.rem(spot + 31 - d, 32)], t2r.at[d])
@@ -216,11 +251,13 @@
     def group_step(g, carry):
         @pl.when(g < GROUPS - 1)
         def _():
-            for i in range(len(fs_dev)):
-                landed(kv.at[core, g + 1, origin(i)], ar_sem.at[g + 1, i])
-            send(kv.at[core, g + 1], kv.at[core, g + 1], cs_sem.at[g + 1], cr_sem.at[g + 1], twin)
-
-        landed(kv.at[other, g], cr_sem.at[g])
+            pass_twin(g + 1)
+
+        @pl.when(g < GROUPS - 2)
+        def _():
+            pass_flip(g + 2)
+
+        complete(g)
         ups, queries, grads = [], [], []
         for a in range(PER):
             h = g * PER + a
@@ -307,11 +344,8 @@
     up_out[...] = whole[:, 256:384]
     for copy in sent + steps:
         copy.wait_send()
-    for g in range(GROUPS):
-        pltpu.make_async_remote_copy(
-            src_ref=kv.at[core, g], dst_ref=kv.at[core, g], send_sem=cs_sem.at[g], recv_sem=cr_sem.at[g],
-            device_id=twin, device_id_type=MESH,
-        ).wait_send()
+    for chunk in [None] + list(range(GROUPS)):
+        left(chunk)
 
 
 def step(*args):
@@ -354,9 +388,9 @@
             pltpu.VMEM((8, 8, PCOLS), BF),
             pltpu.VMEM((2, NX, 8, PCOLS), F32),
             dma((7,)), dma((3,)),
-            dma((GROUPS + 1, 15)), dma((GROUPS + 1, 15)),
+            dma((GROUPS + 1, 7)), dma((GROUPS + 1, 7)), dma((GROUPS + 1,)), dma((GROUPS + 1,)),
             dma((15,)), dma((15,)),
-            dma((GROUPS + 1,)), dma((GROUPS + 1,)),
+            dma((2, GROUPS + 1)), dma((2, GROUPS + 1)),
             dma((15,)), dma((15,)), dma((31,)), dma((31,)),
             dma((4,)), dma((4,)), dma((4, 3)), dma((4, 3)),
             dma((7,)), dma((7,)), dma((7,)), dma((7,)), dma((7,)), dma((7,)),
@@ -364,6 +398,29 @@
         compiler_params=pltpu.CompilerParams(collective_id=0, has_side_effects=True, vmem_limit_bytes=60 * 1024 * 1024),
         name="step",
     )(*args)
+
+
+def place_kernel(seq_ref, down_ref, up_ref, down_out, up_out, seq_out):
+    down_out[...] = down_ref[...]
+    up_out[...] = up_ref[...]
+    for r in range(RESP):
+        seq_out[r] = seq_ref[r, 0]
+
+
+def place_outputs(seq, down, up):
+    vmem = pl.BlockSpec(memory_space=pltpu.VMEM)
+    smem = pl.BlockSpec(memory_space=pltpu.SMEM)
+    return pl.pallas_call(
+        place_kernel,
+        out_shape=(
+            jax.ShapeDtypeStruct((RANK, 256), F32),
+            jax.ShapeDtypeStruct((RANK, HEAD), F32),
+            jax.ShapeDtypeStruct((RESP,), F32),
+        ),
+        in_specs=[smem, vmem, vmem],
+        out_specs=(vmem, vmem, smem),
+        name="place_outputs",
+    )(seq, down, up)
 
 
 def body(
@@ -392,7 +449,8 @@
         frozen_query_rows.reshape(ROWS, HEADS * HEAD),
         output_gradient.reshape(ROWS, HEADS * HEAD),
     )
-    return grad_down_t.T, grad_up, seq[0:RESP, 0]
+    grad_down_t, grad_up, seq_ratio = place_outputs(seq, grad_down_t, grad_up)
+    return grad_down_t.T, grad_up, seq_ratio
 
 
 def solution(mesh):

time: 94.8 us -> 84.8 us (0.89)
  Pallas kernels: 89.7 us -> 83.9 us
  local copies, waits for them, and re-layouts: 4.16 us -> 0 us
    pallas_call x1, Pallas kernels: 89.7 us -> 82.4 us  [step(): pl.pallas_call(step_kernel, out_shape=(jax.ShapeDtypeStruct((8, 128), F32...]
    unnamed x2 -> x0, local copies, waits for them, and re-layouts: 2.85 us -> none
    pallas_call x0 -> x1, Pallas kernels: none -> 1.5 us  [place_outputs(): pl.pallas_call(place_kernel, out_shape=(jax.ShapeDtypeStruct((RANK, 256),...]
    slice x1 -> x0, local copies, waits for them, and re-layouts: 1.31 us -> none  [body(): return (grad_down_t.T, grad_up, seq[0:RESP, 0])]
where the time goes in v3:
time: 84.8 us; the launch traced here: 84.6 us
  Pallas kernels  83.9 us (99%)
    pallas_call x1, Pallas kernels, step(): pl.pallas_call(step_kernel, out_shape=(jax.ShapeDtypeStruct((8, 128), F32...  82.4 us

profile of v3, /device:TPU:1, one launch (start us, length us, event | category | flops | bytes accessed | tf_op | source)
XLA Modules:
  0.0 84.6 jit_solution(11568186970420569592)
XLA Ops:
  0.6 82.4 %step.1 = (f32[8,128]{1,0:T(8,128)}, f32[64,256]{1,0:T(8,128)}, f32[64,128]{1,0:T(8,128)}) custom-call(s32[4]{0:T(128)} %lengths_ref.1, f32[4]{0:T(128)} %win_ref.1, f32[4,64]{1,0:T(4,128)} %bitcast.11, bf16[64,512]{1,0:T(8,128)(2,1)} %k_ref.1, bf16[64,512]{1,0:T(8,128)(2,1)} %v_ref.1, bf16[64,256]{1,0:T(8,128)(2,1)} %bitcast.10, bf16[64,128]{1,0:T(8,128)(2,1)} %up_ref.1, ...), custom_call_target="tpu_custom_call" | custom-call | tf_op jit(solution)/shard_map/step/pallas_call | solution.py:357
  83.1 1.5 %place_outputs.1 = (f32[64,256]{1,0:T(8,128)}, f32[64,128]{1,0:T(8,128)}, f32[4]{0:T(128)}) custom-call(f32[8,128]{1,0:T(8,128)} %get-tuple-element.9.seq_ref, f32[64,256]{1,0:T(8,128)} %get-tuple-element.10.down_ref, f32[64,128]{1,0:T(8,128)} %get-tuple-element.11.up_ref), custom_call_target="tpu_custom_call" | custom-call | tf_op jit(solution)/shard_map/place_outputs/pallas_call | solution.py:413
